TPU v7x, 32 devices: a whole 2x2x4 slice. The times are simulated.
32 devices in a mesh: member: 16 (over z, y, x), domain: 2 (over core).
Axes of the slice: x: 2, y: 2, z: 4, core: 2. Of those that a mesh axis runs over, the one named last changes fastest.
Arguments:
- state: bfloat16 [512, 32768], P('member', 'domain'), may hold values from -6 to 6
- predicted: bfloat16 [512, 65536], P('member', 'domain'), may hold values from -6 to 6
- perturbed: bfloat16 [512, 65536], P('member', 'domain'), may hold values from -6 to 6
- obs_weight: float32 [65536], P('domain'), may hold values from 0.3 to 3
- obs_position: int32 [65536], P('domain'), may hold values from 0 to 63
- row_count: int32 [2, 32], P(None, 'member'), may hold values from 256 to 2048
- row_index: int32 [2, 32, 2048], P('domain', 'member'), may hold values from 0 to 2047, as said below
Outputs:
- updated: bfloat16 [512, 32768], P('member', 'domain')
Inputs may be any that keep to these rules, and one draw needn't show every extreme that they name: `row_index`: for each block, 2048 distinct rows of its pool; only the first row_count of them are used.
All inputs are finite; a program needn't handle non-finite values.
Results may differ from a plain program's by a relative error of at most 0.0054.
Values may be sent and summed in bfloat16 or wider, within the bound.
A program may use at most 128 MiB of HBM per device.

v0:
```python
import jax
import jax.numpy as jnp
from jax import lax
from jax.sharding import PartitionSpec as P

NS_STEPS = 5
SPAN = 2
LANES = 128


def product(left, right):
    return jnp.dot(left, right, precision=lax.Precision.HIGH)


def row_product(left, right):
    return lax.dot_general(
        left, right, (((1,), (1,)), ((), ())), preferred_element_type=jnp.float32
    )


def listed_rows(index_list, row_total, pool_rows):
    places = jnp.arange(index_list.shape[0], dtype=jnp.int32)
    live = places < row_total
    high = (index_list // LANES)[None, :] == jnp.arange(pool_rows // LANES)[:, None]
    low = (index_list % LANES)[None, :] == jnp.arange(LANES)[:, None]
    marks = row_product((high & live[None, :]).astype(jnp.bfloat16), low.astype(jnp.bfloat16))
    return marks.reshape(1, pool_rows)


def newton_weights(gram_sum, cross_sum):
    members = gram_sum.shape[0]
    identity = jnp.eye(members, dtype=jnp.float32)
    spread = jnp.sqrt(jnp.sum(gram_sum * gram_sum))
    start = 2.0 / (2.0 + spread)
    residual = identity - start * (identity + gram_sum)
    total = identity + residual
    for _ in range(NS_STEPS - 1):
        residual = product(residual, residual)
        total = total + product(total, residual)
    return start * product(total, cross_sum)


def per_device(state, predicted, perturbed, obs_weight, obs_position, row_count, row_index):
    pred = lax.all_to_all(predicted, "member", split_axis=1, concat_axis=0, tiled=True)
    pert = lax.all_to_all(perturbed, "member", split_axis=1, concat_axis=0, tiled=True)
    cells = lax.all_to_all(state, "member", split_axis=1, concat_axis=0, tiled=True)
    groups = lax.axis_size("member")
    group_index = lax.axis_index("member")
    tile_index = lax.axis_index("domain")
    members, pool_rows = pred.shape
    blocks = row_index.shape[1]
    block_cells = cells.shape[1] // blocks
    first_block = (tile_index * groups + group_index) * blocks
    counts = lax.dynamic_index_in_dim(row_count, tile_index, 0, keepdims=False)
    weight = lax.dynamic_slice_in_dim(obs_weight, group_index * pool_rows, pool_rows)[None, :]
    place = lax.dynamic_slice_in_dim(obs_position, group_index * pool_rows, pool_rows)[None, :]
    pred_wide = pred.astype(jnp.float32)
    pred_centred = pred_wide - jnp.mean(pred_wide, axis=0, keepdims=True)
    departure = pert.astype(jnp.float32) - pred_wide
    renewed = []
    for number in range(blocks):
        offset = (place - (first_block + number)).astype(jnp.float32) / SPAN
        marks = listed_rows(row_index[0, number], counts[number], pool_rows)
        factor = marks * (weight * (1.0 / (1.0 + offset * offset)))
        scaled = (factor * pred_centred / jnp.sqrt(members - 1.0)).astype(jnp.bfloat16)
        innovation = (factor * departure).astype(jnp.bfloat16)
        gram_sum = row_product(scaled, scaled)
        cross_sum = row_product(scaled, innovation)
        weights = (newton_weights(gram_sum, cross_sum) / jnp.sqrt(members - 1.0)).astype(
            jnp.bfloat16
        )
        values = cells[:, number * block_cells : (number + 1) * block_cells].astype(jnp.float32)
        centred = (values - jnp.mean(values, axis=0, keepdims=True)).astype(jnp.bfloat16)
        change = lax.dot_general(
            weights, centred, (((0,), (0,)), ((), ())), preferred_element_type=jnp.float32
        )
        renewed.append((values + change).astype(jnp.bfloat16))
    return lax.all_to_all(
        jnp.concatenate(renewed, axis=1), "member", split_axis=0, concat_axis=1, tiled=True
    )


def solution(mesh):
    placed = (
        P("member", "domain"),
        P("member", "domain"),
        P("member", "domain"),
        P("domain"),
        P("domain"),
        P(None, "member"),
        P("domain", "member", None),
    )
    return jax.shard_map(
        per_device, mesh=mesh, in_specs=placed, out_specs=P("member", "domain"), check_vma=False
    )
```

profile of v0, /device:TPU:0, one launch (start us, length us, event | category | flops | bytes accessed | tf_op | source)
XLA Modules:
  0.0 209.1 jit_solution(13166296687024615946)
XLA Ops:
  0.0 2.4 %copy.40 = bf16[4,16,8,1024]{3,2,0,1:T(8,128)(2,1)} copy(bf16[4,16,8,1024]{3,2,1,0:T(8,128)(2,1)} %bitcast.96) | data formatting | bytes 2097152 | tf_op jit(solution)/shard_map/all_to_all | solution.py:46
  2.4 8.3 %all-to-all-start = ((bf16[32,16,1024]{2,0,1:T(8,128)(2,1)}), bf16[32,16,1024]{2,0,1:T(8,128)(2,1)S(1)}, u32[]{:S(2)}, u32[]{:S(2)}) async-start(bf16[32,16,1024]{2,0,1:T(8,128)(2,1)} %bitcast.82), calls=%async_computation | async-start | bytes 2097152 | tf_op jit(solution)/shard_map/all_to_all | solution.py:46
  10.8 1.5 copy.39
  12.3 22.9 %all-to-all-done = bf16[32,16,1024]{2,0,1:T(8,128)(2,1)S(1)} async-done(((bf16[32,16,1024]{2,0,1:T(8,128)(2,1)}), bf16[32,16,1024]{2,0,1:T(8,128)(2,1)S(1)}, u32[]{:S(2)}, u32[]{:S(2)}) %all-to-all-start) | async-done | bytes 1048608 | tf_op jit(solution)/shard_map/all_to_all | solution.py:46
  35.2 5.9 %all-to-all-start.1 = ((bf16[32,16,2048]{2,0,1:T(8,128)(2,1)}), bf16[32,16,2048]{2,0,1:T(8,128)(2,1)S(1)}, u32[]{:S(2)}, u32[]{:S(2)}) async-start(bf16[32,16,2048]{2,0,1:T(8,128)(2,1)} %bitcast.84), calls=%async_computation.1 | async-start | bytes 4194304 | tf_op jit(solution)/shard_map/all_to_all | solution.py:44
  41.1 3.2 %copy.38 = bf16[4,16,8,2048]{3,2,0,1:T(8,128)(2,1)} copy(bf16[4,16,8,2048]{3,2,1,0:T(8,128)(2,1)} %bitcast.89) | data formatting | bytes 4194304 | tf_op jit(solution)/shard_map/all_to_all | solution.py:45
  44.2 38.7 %all-to-all-done.1 = bf16[32,16,2048]{2,0,1:T(8,128)(2,1)S(1)} async-done(((bf16[32,16,2048]{2,0,1:T(8,128)(2,1)}), bf16[32,16,2048]{2,0,1:T(8,128)(2,1)S(1)}, u32[]{:S(2)}, u32[]{:S(2)}) %all-to-all-start.1) | async-done | bytes 2097184 | tf_op jit(solution)/shard_map/all_to_all | solution.py:44
  82.9 10.0 %all-to-all-start.2 = ((bf16[32,16,2048]{2,0,1:T(8,128)(2,1)}), bf16[32,16,2048]{2,0,1:T(8,128)(2,1)}, u32[]{:S(2)}, u32[]{:S(2)}) async-start(bf16[32,16,2048]{2,0,1:T(8,128)(2,1)} %bitcast.83), calls=%async_computation.2 | async-start | bytes 4194304 | tf_op jit(solution)/shard_map/all_to_all | solution.py:45
  92.9 0.6 fusion.44
  93.5 0.6 iota_compare_fusion.9
  94.0 0.7 iota_compare_fusion.10
  94.8 1.0 fusion.13
  95.8 1.0 fusion.12
  96.8 1.1 fusion.42
  97.9 1.3 copy.29
  99.1 1.3 copy.30
  101.1 34.4 %all-to-all-done.2 = bf16[32,16,2048]{2,0,1:T(8,128)(2,1)} async-done(((bf16[32,16,2048]{2,0,1:T(8,128)(2,1)}), bf16[32,16,2048]{2,0,1:T(8,128)(2,1)}, u32[]{:S(2)}, u32[]{:S(2)}) %all-to-all-start.2) | async-done | bytes 2097184 | tf_op jit(solution)/shard_map/all_to_all | solution.py:45
  135.5 5.2 %multiply_convert_fusion.1 = (bf16[32,16,2048]{2,0,1:T(8,128)(2,1)}, bf16[32,16,2048]{2,0,1:T(8,128)(2,1)}, bf16[32,16,2048]{2,0,1:T(8,128)(2,1)}, bf16[32,16,2048]{2,0,1:T(8,128)(2,1)S(1)}) fusion(bf16[32,16,2048]{2,0,1:T(8,128)(2,1)S(1)} %all-to-all-done.1, bf16[32,16,2048]{2,0,1:T(8,128)(2,1)} %all-to-all-done.2, f32[2048]{0:T(1024)S(1)} %fusion.13, ...), kind=kLoop, calls=%fused_computation.10 | loop fusion | flops 14680064 | bytes 12607488 | tf_op jit(solution)/shard_map/convert_element_type | solution.py:66
  140.8 2.0 multiply_reduce_fusion.1
  143.5 1.1 fusion.18
  144.6 2.0 convolution_add_fusion.7
  146.6 1.0 fusion.45
  147.7 0.5 copy-done.3
  148.2 2.1 multiply_reduce_fusion
  151.1 1.1 fusion.19
  152.2 1.1 convolution_add_fusion.3
  153.3 1.0 fusion.49
  154.3 1.0 fusion.46
  155.5 1.0 convolution_add_fusion.6
  156.6 1.0 fusion.47
  157.7 1.3 convolution_add_fusion.5
  159.0 0.4 copy-done.5
  159.4 1.3 fusion.48
  161.0 0.6 copy-done.4
  161.6 1.3 fusion.52
  162.9 1.0 fusion.50
  163.9 1.1 convolution_add_fusion.2
  165.0 1.0 fusion.51
  166.1 1.0 convolution_add_fusion.1
  167.1 1.1 convolution_add_fusion.4
  168.2 1.0 fusion.10
  169.3 0.5 fusion.8
  169.8 1.0 convolution_add_fusion
  170.8 1.0 fusion.11
  171.9 0.5 fusion.9
  172.4 0.5 copy.27
  173.0 35.1 %all_to_all.64 = bf16[16,32,1024]{2,1,0:T(8,128)(2,1)S(1)} all-to-all(bf16[16,32,1024]{2,1,0:T(8,128)(2,1)S(1)} %bitcast.86), channel_id=1, replica_groups=mesh['member'=16,'domain'=2] {'member'}, dimensions={0} | all-to-all | bytes 2097152 | tf_op jit(solution)/shard_map/all_to_all | solution.py:78
  208.1 1.1 copy.34
  (28 shorter events, 1.3 us)
Async XLA Ops:
  0.0 92.9 %copy-start = (s32[2,2]{1,0:T(2,128)S(1)}, s32[2,2]{1,0:T(2,128)}, u32[]{:S(2)}) copy-start(s32[2,2]{1,0:T(2,128)} %param.12) | copy-start | bytes 52
  0.0 10.8 %copy-start.1 = (bf16[32,32768]{1,0:T(8,128)(2,1)S(1)}, bf16[32,32768]{1,0:T(8,128)(2,1)}, u32[]{:S(2)}) copy-start(bf16[32,32768]{1,0:T(8,128)(2,1)} %param.8) | copy-start | bytes 6291460
  2.4 32.7 %all-to-all-start = ((bf16[32,16,1024]{2,0,1:T(8,128)(2,1)}), bf16[32,16,1024]{2,0,1:T(8,128)(2,1)S(1)}, u32[]{:S(2)}, u32[]{:S(2)}) async-start(bf16[32,16,1024]{2,0,1:T(8,128)(2,1)} %bitcast.82), calls=%async_computation | async-start | bytes 2097152 | tf_op jit(solution)/shard_map/all_to_all | solution.py:46
  35.2 47.7 %all-to-all-start.1 = ((bf16[32,16,2048]{2,0,1:T(8,128)(2,1)}), bf16[32,16,2048]{2,0,1:T(8,128)(2,1)S(1)}, u32[]{:S(2)}, u32[]{:S(2)}) async-start(bf16[32,16,2048]{2,0,1:T(8,128)(2,1)} %bitcast.84), calls=%async_computation.1 | async-start | bytes 4194304 | tf_op jit(solution)/shard_map/all_to_all | solution.py:44
  82.9 11.8 %copy-start.9 = (s32[1,2,2048]{2,1,0:T(2,128)S(1)}, s32[1,2,2048]{2,1,0:T(2,128)}, u32[]{:S(2)}) copy-start(s32[1,2,2048]{2,1,0:T(2,128)} %param.13) | copy-start | bytes 49156
  82.9 52.6 %all-to-all-start.2 = ((bf16[32,16,2048]{2,0,1:T(8,128)(2,1)}), bf16[32,16,2048]{2,0,1:T(8,128)(2,1)}, u32[]{:S(2)}, u32[]{:S(2)}) async-start(bf16[32,16,2048]{2,0,1:T(8,128)(2,1)} %bitcast.83), calls=%async_computation.2 | async-start | bytes 4194304 | tf_op jit(solution)/shard_map/all_to_all | solution.py:45
  140.8 2.0 copy-start.6
  146.6 1.6 copy-start.3
  154.3 1.2 copy-start.8
  156.6 2.4 %copy-start.7 = (bf16[32,16,2048]{2,0,1:T(8,128)(2,1)S(1)}, bf16[32,16,2048]{2,0,1:T(8,128)(2,1)}, u32[]{:S(2)}) copy-start(bf16[32,16,2048]{2,0,1:T(8,128)(2,1)} %copy-done.6) | copy-start | bytes 6291460
  157.6 1.7 copy-start.5
  159.4 1.6 copy-start.2
  159.4 2.2 %copy-start.4 = (bf16[32,16,2048]{2,0,1:T(8,128)(2,1)S(1)}, bf16[32,16,2048]{2,0,1:T(8,128)(2,1)}, u32[]{:S(2)}) copy-start(bf16[32,16,2048]{2,0,1:T(8,128)(2,1)} %get-tuple-element.7) | copy-start | bytes 6291460
where the time goes:
time: 210 us; the launch traced here: 209 us
  waiting for transfers between devices  96 us (46%)
  blocking collectives  35.1 us (17%)
  matrix products  29.9 us (14%)
  starting transfers between devices  24.2 us (12%)
  local copies, waits for them, and re-layouts  14.9 us (7%)
  other arithmetic  7.25 us (3%)
    all_to_all x1, waiting for transfers between devices, per_device(): lax.all_to_all(predicted, 'member', split_axis=1, concat_axis=0, tiled=True)  38.7 us
    all_to_all x1, blocking collectives, per_device(): lax.all_to_all(jnp.concatenate(renewed, axis=1), 'member', split_axis=0,...  35.1 us
    all_to_all x1, waiting for transfers between devices, per_device(): lax.all_to_all(perturbed, 'member', split_axis=1, concat_axis=0, tiled=True)  34.4 us
    all_to_all x1, waiting for transfers between devices, per_device(): lax.all_to_all(state, 'member', split_axis=1, concat_axis=0, tiled=True)  22.9 us
    dot_general x18, matrix products, product(): return jnp.dot(left, right, precision=lax.Precision.HIGH)  20.2 us
    all_to_all x1, starting transfers between devices, per_device(): lax.all_to_all(perturbed, 'member', split_axis=1, concat_axis=0, tiled=True)  9.95 us
    dot_general x6, matrix products, row_product(): lax.dot_general(left, right, (((1,), (1,)), ((), ())), preferred_element_...  8.69 us
    all_to_all x1, starting transfers between devices, per_device(): lax.all_to_all(state, 'member', split_axis=1, concat_axis=0, tiled=True)  8.34 us
  transfers between devices with their start and end apart: 3, of which 3 were waited for; matrix products, arithmetic and copies ran while one was open for 6% of the time, Pallas kernels for 0%

commit v1 on v0

--- a/solution.py
+++ b/solution.py
@@ -2,6 +2,7 @@
 import jax.numpy as jnp
 from jax import lax
 from jax.sharding import PartitionSpec as P
+from jax.lax import all_to_all, axis_size
 
 NS_STEPS = 5
 SPAN = 2
@@ -75,8 +76,14 @@
             weights, centred, (((0,), (0,)), ((), ())), preferred_element_type=jnp.float32
         )
         renewed.append((values + change).astype(jnp.bfloat16))
-    return lax.all_to_all(
-        jnp.concatenate(renewed, axis=1), "member", split_axis=0, concat_axis=1, tiled=True
+    return jnp.concatenate(
+        all_to_all(
+            jnp.stack(jnp.split(jnp.concatenate(renewed, axis=1), axis_size("member"), 0), 0),
+            "member",
+            split_axis=0,
+            concat_axis=0,
+        ),
+        1,
     )
 
 

time: 210 us -> 222 us (1.057)
  local copies, waits for them, and re-layouts: 14.9 us -> 24.8 us
    another operation x0 -> x17, local copies, waits for them, and re-layouts: none -> 9.8 us  [per_device(): jnp.stack(jnp.split(jnp.concatenate(renewed, axis=1), axis_size('member')...]
    unnamed x22 -> x45, local copies, waits for them, and re-layouts: 4.58 us -> 5.23 us
where the time goes in v1:
time: 222 us; the launch traced here: 221 us
  waiting for transfers between devices  96 us (43%)
  blocking collectives  35.2 us (16%)
  matrix products  29.8 us (13%)
  local copies, waits for them, and re-layouts  24.8 us (11%)
  starting transfers between devices  24.2 us (11%)
  other arithmetic  9.22 us (4%)
    all_to_all x1, waiting for transfers between devices, per_device(): lax.all_to_all(predicted, 'member', split_axis=1, concat_axis=0, tiled=True)  38.7 us
    all_to_all x1, blocking collectives, per_device(): all_to_all(jnp.stack(jnp.split(jnp.concatenate(renewed, axis=1), axis_siz...  35.2 us
    all_to_all x1, waiting for transfers between devices, per_device(): lax.all_to_all(perturbed, 'member', split_axis=1, concat_axis=0, tiled=True)  34.4 us
    all_to_all x1, waiting for transfers between devices, per_device(): lax.all_to_all(state, 'member', split_axis=1, concat_axis=0, tiled=True)  22.9 us
    dot_general x18, matrix products, product(): return jnp.dot(left, right, precision=lax.Precision.HIGH)  20.2 us
    all_to_all x1, starting transfers between devices, per_device(): lax.all_to_all(perturbed, 'member', split_axis=1, concat_axis=0, tiled=True)  9.95 us
    another operation x17, local copies, waits for them, and re-layouts, per_device(): jnp.stack(jnp.split(jnp.concatenate(renewed, axis=1), axis_size('member')...  9.8 us
    dot_general x6, matrix products, row_product(): lax.dot_general(left, right, (((1,), (1,)), ((), ())), preferred_element_...  8.64 us
  transfers between devices with their start and end apart: 3, of which 3 were waited for; matrix products, arithmetic and copies ran while one was open for 6% of the time, Pallas kernels for 0%

profile of v1, /device:TPU:0, one launch (start us, length us, event | category | flops | bytes accessed | tf_op | source)
XLA Modules:
  0.0 221.2 jit_solution(10573958920354815562)
XLA Ops:
  0.0 2.4 %copy.75 = bf16[4,16,8,1024]{3,2,0,1:T(8,128)(2,1)} copy(bf16[4,16,8,1024]{3,2,1,0:T(8,128)(2,1)} %bitcast.126) | data formatting | bytes 2097152 | tf_op jit(solution)/shard_map/all_to_all | solution.py:47
  2.4 8.3 %all-to-all-start = ((bf16[32,16,1024]{2,0,1:T(8,128)(2,1)}), bf16[32,16,1024]{2,0,1:T(8,128)(2,1)S(1)}, u32[]{:S(2)}, u32[]{:S(2)}) async-start(bf16[32,16,1024]{2,0,1:T(8,128)(2,1)} %bitcast.113), calls=%async_computation | async-start | bytes 2097152 | tf_op jit(solution)/shard_map/all_to_all | solution.py:47
  10.8 1.5 copy.74
  12.3 22.9 %all-to-all-done = bf16[32,16,1024]{2,0,1:T(8,128)(2,1)S(1)} async-done(((bf16[32,16,1024]{2,0,1:T(8,128)(2,1)}), bf16[32,16,1024]{2,0,1:T(8,128)(2,1)S(1)}, u32[]{:S(2)}, u32[]{:S(2)}) %all-to-all-start) | async-done | bytes 1048608 | tf_op jit(solution)/shard_map/all_to_all | solution.py:47
  35.2 5.9 %all-to-all-start.1 = ((bf16[32,16,2048]{2,0,1:T(8,128)(2,1)}), bf16[32,16,2048]{2,0,1:T(8,128)(2,1)S(1)}, u32[]{:S(2)}, u32[]{:S(2)}) async-start(bf16[32,16,2048]{2,0,1:T(8,128)(2,1)} %bitcast.115), calls=%async_computation.1 | async-start | bytes 4194304 | tf_op jit(solution)/shard_map/all_to_all | solution.py:45
  41.1 3.2 %copy.73 = bf16[4,16,8,2048]{3,2,0,1:T(8,128)(2,1)} copy(bf16[4,16,8,2048]{3,2,1,0:T(8,128)(2,1)} %bitcast.119) | data formatting | bytes 4194304 | tf_op jit(solution)/shard_map/all_to_all | solution.py:46
  44.2 38.7 %all-to-all-done.1 = bf16[32,16,2048]{2,0,1:T(8,128)(2,1)S(1)} async-done(((bf16[32,16,2048]{2,0,1:T(8,128)(2,1)}), bf16[32,16,2048]{2,0,1:T(8,128)(2,1)S(1)}, u32[]{:S(2)}, u32[]{:S(2)}) %all-to-all-start.1) | async-done | bytes 2097184 | tf_op jit(solution)/shard_map/all_to_all | solution.py:45
  82.9 10.0 %all-to-all-start.2 = ((bf16[32,16,2048]{2,0,1:T(8,128)(2,1)}), bf16[32,16,2048]{2,0,1:T(8,128)(2,1)}, u32[]{:S(2)}, u32[]{:S(2)}) async-start(bf16[32,16,2048]{2,0,1:T(8,128)(2,1)} %bitcast.114), calls=%async_computation.2 | async-start | bytes 4194304 | tf_op jit(solution)/shard_map/all_to_all | solution.py:46
  93.5 0.7 iota_compare_fusion.9
  94.8 1.0 fusion.13
  95.8 1.0 fusion.12
  96.8 1.1 fusion.73
  97.9 1.3 copy.64
  99.1 1.3 copy.65
  101.1 34.4 %all-to-all-done.2 = bf16[32,16,2048]{2,0,1:T(8,128)(2,1)} async-done(((bf16[32,16,2048]{2,0,1:T(8,128)(2,1)}), bf16[32,16,2048]{2,0,1:T(8,128)(2,1)}, u32[]{:S(2)}, u32[]{:S(2)}) %all-to-all-start.2) | async-done | bytes 2097184 | tf_op jit(solution)/shard_map/all_to_all | solution.py:46
  135.5 5.3 %multiply_convert_fusion = (bf16[32,16,2048]{2,0,1:T(8,128)(2,1)}, bf16[32,16,2048]{2,0,1:T(8,128)(2,1)}, bf16[32,16,2048]{2,0,1:T(8,128)(2,1)S(1)}, bf16[32,16,2048]{2,0,1:T(8,128)(2,1)}) fusion(bf16[32,16,2048]{2,0,1:T(8,128)(2,1)S(1)} %all-to-all-done.1, bf16[32,16,2048]{2,0,1:T(8,128)(2,1)} %all-to-all-done.2, f32[2048]{0:T(1024)S(1)} %fusion.12, ...), kind=kLoop, calls=%fused_computation.9 | loop fusion | flops 14680064 | bytes 12607488 | tf_op jit(solution)/shard_map/convert_element_type | solution.py:67
  140.8 2.0 multiply_reduce_fusion.1
  143.5 1.1 fusion.18
  144.6 2.0 convolution_add_fusion.7
  146.6 1.0 fusion.76
  148.2 2.0 multiply_reduce_fusion
  151.0 1.1 fusion.19
  152.0 1.1 convolution_add_fusion.3
  153.1 1.0 fusion.80
  154.2 1.0 fusion.77
  155.4 1.0 convolution_add_fusion.6
  156.5 1.0 fusion.78
  157.5 1.3 convolution_add_fusion.5
  159.2 1.3 fusion.79
  160.5 1.0 fusion.81
  161.6 1.1 convolution_add_fusion.2
  162.7 1.0 fusion.82
  163.7 1.1 convolution_add_fusion.1
  164.8 0.6 copy-done.2
  165.5 1.3 fusion.83
  166.7 1.1 convolution_add_fusion.4
  167.8 1.0 fusion.10
  169.4 1.1 convolution_add_fusion
  170.5 1.0 fusion.11
  172.5 1.6 fusion.60
  174.3 1.7 copy.48
  176.0 1.7 copy.49
  177.7 1.7 copy.50
  179.3 1.7 copy.51
  181.0 1.7 copy.52
  183.9 0.8 constant_dynamic-update-slice_fusion.14
  185.0 35.2 %all_to_all.50 = bf16[16,32,1024]{2,1,0:T(8,128)(2,1)S(1)} all-to-all(bf16[16,32,1024]{2,1,0:T(8,128)(2,1)S(1)} %constant_dynamic-update-slice_fusion), channel_id=1, replica_groups=mesh['member'=16,'domain'=2] {'member'}, dimensions={0} | all-to-all | bytes 2097152 | tf_op jit(solution)/shard_map/all_to_all | solution.py:80
  220.1 1.1 copy.69
  (68 shorter events, 6.0 us)
Async XLA Ops:
  0.0 92.9 %copy-start = (s32[2,2]{1,0:T(2,128)S(1)}, s32[2,2]{1,0:T(2,128)}, u32[]{:S(2)}) copy-start(s32[2,2]{1,0:T(2,128)} %param.12) | copy-start | bytes 52
  0.0 10.8 %copy-start.1 = (bf16[32,32768]{1,0:T(8,128)(2,1)S(1)}, bf16[32,32768]{1,0:T(8,128)(2,1)}, u32[]{:S(2)}) copy-start(bf16[32,32768]{1,0:T(8,128)(2,1)} %param.8) | copy-start | bytes 6291460
  2.4 32.7 %all-to-all-start = ((bf16[32,16,1024]{2,0,1:T(8,128)(2,1)}), bf16[32,16,1024]{2,0,1:T(8,128)(2,1)S(1)}, u32[]{:S(2)}, u32[]{:S(2)}) async-start(bf16[32,16,1024]{2,0,1:T(8,128)(2,1)} %bitcast.113), calls=%async_computation | async-start | bytes 2097152 | tf_op jit(solution)/shard_map/all_to_all | solution.py:47
  35.2 47.7 %all-to-all-start.1 = ((bf16[32,16,2048]{2,0,1:T(8,128)(2,1)}), bf16[32,16,2048]{2,0,1:T(8,128)(2,1)S(1)}, u32[]{:S(2)}, u32[]{:S(2)}) async-start(bf16[32,16,2048]{2,0,1:T(8,128)(2,1)} %bitcast.115), calls=%async_computation.1 | async-start | bytes 4194304 | tf_op jit(solution)/shard_map/all_to_all | solution.py:45
  82.9 11.8 %copy-start.13 = (s32[1,2,2048]{2,1,0:T(2,128)S(1)}, s32[1,2,2048]{2,1,0:T(2,128)}, u32[]{:S(2)}) copy-start(s32[1,2,2048]{2,1,0:T(2,128)} %param.13) | copy-start | bytes 49156
  82.9 52.6 %all-to-all-start.2 = ((bf16[32,16,2048]{2,0,1:T(8,128)(2,1)}), bf16[32,16,2048]{2,0,1:T(8,128)(2,1)}, u32[]{:S(2)}, u32[]{:S(2)}) async-start(bf16[32,16,2048]{2,0,1:T(8,128)(2,1)} %bitcast.114), calls=%async_computation.2 | async-start | bytes 4194304 | tf_op jit(solution)/shard_map/all_to_all | solution.py:46
  140.8 2.0 copy-start.6
  146.6 1.6 copy-start.3
  154.2 1.2 copy-start.8
  156.5 2.4 %copy-start.7 = (bf16[32,16,2048]{2,0,1:T(8,128)(2,1)S(1)}, bf16[32,16,2048]{2,0,1:T(8,128)(2,1)}, u32[]{:S(2)}) copy-start(bf16[32,16,2048]{2,0,1:T(8,128)(2,1)} %copy-done.6) | copy-start | bytes 6291460
  157.5 1.7 copy-start.5
  162.7 2.2 copy-start.4
  163.7 1.7 copy-start.2
  183.1 1.7 copy-start.12
  183.1 1.7 copy-start.11
  183.1 1.7 copy-start.10
  183.1 1.7 copy-start.9
